TPU v7x, 32 devices: a whole 2x2x4 slice. The times are simulated.
32 devices in a mesh: mom: 8 (over z, core), bond: 4 (over y, x).
Axes of the slice: x: 2, y: 2, z: 4, core: 2. Of those that a mesh axis runs over, the one named last changes fastest.
Arguments:
- vertex: bfloat16 [3, 256, 512, 512], P(None, ('mom', 'bond')), may hold values from -6 to 6
- loop_matrix: bfloat16 [3, 256, 512, 512], P(None, ('mom', 'bond')), may hold values from -0.01171875 to 0.01171875
- own_mix: float32 [3, 3], replicated, may hold values from -4 to 4
- cross_mix: float32 [3, 3], replicated, may hold values from -4 to 4
- shells: int32 [512], replicated, may hold values from 0 to 4
- partner: int32 [512], replicated, may hold values from 0 to 511, as said below
- grid_index: int32 [256], replicated, may hold values from 0 to 255, each once
Outputs:
- flowed: bfloat16 [3, 256, 512, 512], P(None, ('mom', 'bond'))
Inputs may be any that keep to these rules, and one draw needn't show every extreme that they name: partner[partner[a]] = a and partner[a] != a for every bond a; partner[a] // 64 = (a // 64 + 512 // 128) % 8. `grid_index`: each grid point appears once; point k has coordinates (k // 16, k % 16).
All inputs are finite; a program needn't handle non-finite values.
Results may differ from a plain program's by a relative error of at most 0.007.
Values may be sent and summed in bfloat16 or wider, within the bound.
A program may use at most 256 MiB of HBM per device.

v0:
```python
import functools
import math

import jax
import jax.numpy as jnp
from jax import lax
from jax.experimental import pallas as pl
from jax.experimental.layout import Layout, with_layout_constraint
from jax.experimental.pallas import tpu as pltpu
from jax.sharding import PartitionSpec as P

LANES = 128
PAIR = 2
ROWS = 2
VMEM_LIMIT = 58 * 1024 * 1024
AXES = ("mom", "bond")


def cas_table(grid_index, negate):
    count = grid_index.shape[0]
    side = math.isqrt(count)
    points = jnp.arange(count, dtype=jnp.int32)
    disp_x = points // side
    disp_y = points % side
    wave_x = grid_index // side
    wave_y = grid_index % side
    phases = (disp_x[:, None] * wave_x[None, :] + disp_y[:, None] * wave_y[None, :]) % side
    if negate:
        phases = (side - phases) % side
    angles = phases.astype(jnp.float32) * (2.0 * math.pi / side)
    return (jnp.cos(angles) + jnp.sin(angles)).astype(jnp.bfloat16)


def cycle_index(count):
    side = math.isqrt(count)
    points = jnp.arange(count, dtype=jnp.int32)
    centre_x = (points // side + side // 2) % side - side // 2
    centre_y = (points % side + side // 2) % side - side // 2
    return jnp.maximum(jnp.abs(centre_x), jnp.abs(centre_y))


def dot(a, b):
    return jnp.dot(a, b, preferred_element_type=jnp.float32)


def product_kernel(mom_local, places, vertex_ref, loop_ref, pick_ref, spread_ref, *refs):
    base_ref, send_ref, token_ref, wide_ref = refs[-4:]
    step = pl.program_id(1)
    token_ref[...] = jnp.zeros_like(token_ref)
    vertex = vertex_ref[0, 0]
    bonds = vertex.shape[0]
    half = bonds // 2
    group = half // places
    half_product = dot(vertex, loop_ref[0, 0]).astype(jnp.bfloat16)
    product = dot(half_product, vertex)
    base_ref[0, 0] = (product + vertex.astype(jnp.float32)).astype(jnp.bfloat16)
    rounded = product.astype(jnp.bfloat16)
    left = rounded[:, :half]
    right = dot(rounded[:, half:], spread_ref[...]).astype(jnp.bfloat16)
    for side, part in enumerate((left, right)):
        upper = dot(pick_ref[...], part[half:])
        lower = part[:half].astype(jnp.float32)
        for lane in range(half // LANES):
            at = side * (half // LANES) + lane
            cols = slice(lane * LANES, (lane + 1) * LANES)
            if mom_local == 1:
                wide_ref[at, :half] = lower[:, cols]
                wide_ref[at, half:] = upper[:, cols]
            else:
                wide_ref[at, pl.ds(step, half, stride=mom_local), :] = lower[:, cols]
                wide_ref[at, pl.ds(half * mom_local + step, half, stride=mom_local), :] = upper[:, cols]

    @pl.when(step == mom_local - 1)
    def _():
        for at in range(bonds // LANES):
            cols = slice(at * LANES, (at + 1) * LANES)
            for side in range(2):
                piece = wide_ref[at, side * half * mom_local : (side + 1) * half * mom_local]
                send_ref[:, 0, side, :, :, cols] = piece.reshape(places, group, mom_local, LANES).astype(jnp.bfloat16)


def first_product_kernel(places, vertex_ref, loop_ref, pick_ref, spread_ref, base_ref, send_ref, token_ref):
    token_ref[...] = jnp.zeros_like(token_ref)
    bonds = vertex_ref.shape[-1]
    half = bonds // 2
    group = half // places
    for n in range(vertex_ref.shape[1]):
        vertex = vertex_ref[0, n]
        half_product = dot(vertex, loop_ref[0, n]).astype(jnp.bfloat16)
        product = dot(half_product, vertex)
        base_ref[0, n] = (product + vertex.astype(jnp.float32)).astype(jnp.bfloat16)
        rounded = product.astype(jnp.bfloat16)
        left = rounded[:, :half]
        right = dot(rounded[:, half:], spread_ref[...]).astype(jnp.bfloat16)
        for side, part in enumerate((left, right)):
            cols = slice(side * half, (side + 1) * half)
            lower = part[:half].astype(jnp.float32)
            upper = dot(pick_ref[...], part[half:])
            send_ref[:, 0, n, 0, :, cols] = lower.reshape(places, group, half).astype(jnp.bfloat16)
            send_ref[:, 0, n, 1, :, cols] = upper.reshape(places, group, half).astype(jnp.bfloat16)


def lattice_kernel(sizes, targets, own_ref, cross_ref, plus_ref, minus_ref, back_ref, cycle_ref, reach_ref, *refs):
    received = [(refs[k], n) for k, size in enumerate(sizes) for n in range(size)]
    send_ref = refs[-1]
    places, _, _, _, mom_local, bonds = send_ref.shape
    count = places * mom_local
    half = bonds // 2
    for row in range(send_ref.shape[3]):
        blocks = [
            [
                ref[:, n, side, row].astype(jnp.float32).reshape(count, bonds).astype(jnp.bfloat16)
                for side in range(2)
            ]
            for ref, n in received
        ]
        for side in range(2):
            mixed = [None] * len(targets)
            for c in range(len(received)):
                own = dot(plus_ref[...], blocks[c][side])
                crossed = dot(minus_ref[...], blocks[c][1 - side])
                crossed = jnp.concatenate([crossed[:, half:], crossed[:, :half]], axis=1)
                for k, d in enumerate(targets):
                    term = own_ref[d, c] * own + cross_ref[d, c] * crossed
                    mixed[k] = term if c == 0 else mixed[k] + term
            kept = cycle_ref[...] <= reach_ref[side, row]
            for k in range(len(targets)):
                projected = jnp.where(kept, mixed[k], 0.0).astype(jnp.bfloat16)
                returned = dot(back_ref[...], projected)
                send_ref[:, k, side, row] = returned.reshape(places, mom_local, bonds).astype(jnp.bfloat16)


def finish_kernel(mom_local, base_ref, received_ref, pick_ref, spread_ref, out_ref, wide_ref):
    step = pl.program_id(1)
    places, _, _, group, _, bonds = received_ref.shape
    half = bonds // 2

    @pl.when(step == 0)
    def _():
        for at in range(bonds // LANES):
            cols = slice(at * LANES, (at + 1) * LANES)
            for side in range(2):
                piece = received_ref[:, 0, side, :, :, cols].astype(jnp.float32)
                wide_ref[at, side * half * mom_local : (side + 1) * half * mom_local] = piece.reshape(
                    half * mom_local, LANES
                )

    def rows_of(at):
        if mom_local == 1:
            return wide_ref[at]
        return wide_ref[at, pl.ds(step, bonds, stride=mom_local), :]

    tiles = half // LANES
    left = jnp.concatenate([rows_of(at) for at in range(tiles)], axis=1)
    right = jnp.concatenate([rows_of(at) for at in range(tiles, 2 * tiles)], axis=1)
    right = dot(right.astype(jnp.bfloat16), pick_ref[...])
    for side, part in enumerate((left, right)):
        cols = slice(side * half, (side + 1) * half)
        lower = part[:half]
        upper = dot(spread_ref[...], part[half:].astype(jnp.bfloat16))
        out_ref[0, 0, :half, cols] = (base_ref[0, 0, :half, cols].astype(jnp.float32) + lower).astype(jnp.bfloat16)
        out_ref[0, 0, half:, cols] = (base_ref[0, 0, half:, cols].astype(jnp.float32) + upper).astype(jnp.bfloat16)


def last_finish_kernel(base_ref, received_ref, pick_ref, spread_ref, out_ref):
    bonds = base_ref.shape[-1]
    half = bonds // 2
    for n in range(base_ref.shape[1]):
        for side in range(2):
            cols = slice(side * half, (side + 1) * half)
            lower = received_ref[:, 0, n, 0, :, cols].astype(jnp.float32).reshape(half, half)
            upper = received_ref[:, 0, n, 1, :, cols].astype(jnp.float32).reshape(half, half).astype(jnp.bfloat16)
            if side:
                lower = dot(lower.astype(jnp.bfloat16), pick_ref[...])
                upper = dot(upper, pick_ref[...]).astype(jnp.bfloat16)
            upper = dot(spread_ref[...], upper)
            out_ref[0, n, :half, cols] = (base_ref[0, n, :half, cols].astype(jnp.float32) + lower).astype(jnp.bfloat16)
            out_ref[0, n, half:, cols] = (base_ref[0, n, half:, cols].astype(jnp.float32) + upper).astype(jnp.bfloat16)


def whole(shape):
    return pl.BlockSpec(shape, lambda *steps: (0,) * len(shape))


def params(axes):
    return pltpu.CompilerParams(dimension_semantics=("arbitrary",) * axes, vmem_limit_bytes=VMEM_LIMIT)


def per_device(vertex, loop_matrix, own_mix, cross_mix, shells, partner, grid_index):
    places = lax.axis_size("mom") * lax.axis_size("bond")
    place = lax.axis_index("mom") * lax.axis_size("bond") + lax.axis_index("bond")
    channels, mom_local, bonds, _ = vertex.shape
    count = grid_index.shape[0]
    half = bonds // 2
    group = half // places
    tiles = bonds // LANES
    bf16 = jnp.bfloat16
    first = list(range(channels))
    send_groups = [first[:1], first[1:]]
    back_groups = [first[:-1], first[-1:]]

    lower_partner = partner[:half] - half
    uppers = jnp.arange(half, dtype=jnp.int32)
    pick = (lower_partner[:, None] == uppers[None, :]).astype(bf16)
    spread = pick.T

    wide = pltpu.VMEM((tiles, bonds * mom_local, LANES), jnp.float32)
    square = (half, half)
    matmul = 2 * mom_local * bonds**3
    field_bytes = 2 * mom_local * bonds * bonds
    field = jax.ShapeDtypeStruct(vertex.shape, bf16)
    token_shape = jax.ShapeDtypeStruct((8, LANES), jnp.float32)

    def flow(members):
        return jax.ShapeDtypeStruct((places, members, 2, group, mom_local, bonds), bf16)

    def one_flow():
        return pl.BlockSpec((places, 1, 2, group, mom_local, bonds), lambda c, i: (0, c, 0, 0, 0, 0))

    def matrix_at(start):
        return pl.BlockSpec((1, 1, bonds, bonds), lambda c, i: (c + start, i, 0, 0))

    def exchange(outgoing):
        return lax.all_to_all(outgoing, AXES, split_axis=0, concat_axis=0, tiled=True)

    pair = PAIR if mom_local % PAIR == 0 else 1
    plain = jax.ShapeDtypeStruct((places, 1, mom_local, 2, group, bonds), bf16)
    plain_block = pl.BlockSpec((places, 1, pair, 2, group, bonds), lambda i: (0, 0, i, 0, 0, 0))

    def pair_at(start):
        return pl.BlockSpec((1, pair, bonds, bonds), lambda i: (start, i, 0, 0))

    base, outgoing, token = pl.pallas_call(
        functools.partial(first_product_kernel, places),
        grid=(mom_local // pair,),
        in_specs=[pair_at(0), pair_at(0), whole(square), whole(square)],
        out_specs=[pair_at(0), plain_block, whole(token_shape.shape)],
        out_shape=[field, plain, token_shape],
        compiler_params=params(1),
        cost_estimate=pl.CostEstimate(flops=5 * matmul // 2, bytes_accessed=4 * field_bytes, transcendentals=0),
        name="product_first",
    )(vertex, loop_matrix, pick, spread)
    whole_rows = with_layout_constraint(exchange(outgoing), Layout(major_to_minor=tuple(range(6))))
    arrived = [whole_rows.transpose(0, 1, 3, 4, 2, 5)]
    for members in send_groups[1:]:
        matrix = matrix_at(members[0])
        size = len(members)
        base, outgoing, _ = pl.pallas_call(
            functools.partial(product_kernel, mom_local, places),
            grid=(size, mom_local),
            in_specs=[matrix, matrix, whole(square), whole(square)]
            + [pl.BlockSpec(memory_space=pl.ANY)],
            out_specs=[matrix, one_flow(), whole(token_shape.shape)],
            out_shape=[field, flow(size), token_shape],
            input_output_aliases={4: 0},
            scratch_shapes=[wide],
            compiler_params=params(2),
            cost_estimate=pl.CostEstimate(
                flops=5 * size * matmul // 2, bytes_accessed=4 * size * field_bytes, transcendentals=0
            ),
            name="product_%d" % members[0],
        )(vertex, loop_matrix, pick, spread, base)
        arrived.append(exchange(outgoing))

    shells, partner, grid_index, own_mix, cross_mix, _ = lax.optimization_barrier(
        (shells, partner, grid_index, own_mix, cross_mix, token)
    )
    plus_table = cas_table(grid_index, False)
    minus_table = cas_table(grid_index, True)
    back_table = plus_table.T
    cycle = cycle_index(count)[:, None]
    shell_order = jnp.concatenate([shells[:half], jnp.take(shells, partner[:half])])
    shell_rows = lax.dynamic_slice_in_dim(shell_order.reshape(2, half), place * group, group, axis=1)
    reach = (shell_rows[:, :, None] + shell_order[None, None, :]).reshape(2, group, 1, bonds)
    own_scaled = own_mix * (1.0 / count)
    cross_scaled = cross_mix * (1.0 / count)

    rows = ROWS if group % ROWS == 0 else 1

    def row_block(members):
        return pl.BlockSpec((places, members, 2, rows, mom_local, bonds), lambda i: (0, 0, 0, i, 0, 0))

    table = whole((count, count))
    scalars = pl.BlockSpec(memory_space=pltpu.SMEM)
    sizes = [len(members) for members in send_groups]
    finished, earlier = [], []
    for members in back_groups:
        size = len(members)
        outgoing = pl.pallas_call(
            functools.partial(lattice_kernel, sizes, members),
            grid=(group // rows,),
            in_specs=[
                scalars,
                scalars,
                table,
                table,
                table,
                whole((count, 1)),
                pl.BlockSpec((2, rows, 1, bonds), lambda i: (0, i, 0, 0)),
            ]
            + [row_block(n) for n in sizes]
            + [pl.BlockSpec(memory_space=pl.ANY)] * len(earlier),
            out_specs=row_block(size),
            out_shape=flow(size),
            compiler_params=params(1),
            cost_estimate=pl.CostEstimate(
                flops=(2 * channels + size) * 2 * count * count * 2 * group * bonds,
                bytes_accessed=(channels + size) * field_bytes,
                transcendentals=0,
            ),
            name="lattice_%d" % members[0],
        )(own_scaled, cross_scaled, plus_table, minus_table, back_table, cycle, reach, *arrived, *earlier)
        earlier = [outgoing]
        if members is back_groups[-1]:
            outgoing = outgoing.transpose(0, 1, 4, 2, 3, 5)
        finished.append(exchange(outgoing))

    for members, received in zip(back_groups[:-1], finished[:-1]):
        matrix = matrix_at(members[0])
        size = len(members)
        base = pl.pallas_call(
            functools.partial(finish_kernel, mom_local),
            grid=(size, mom_local),
            in_specs=[matrix, one_flow(), whole(square), whole(square)],
            out_specs=matrix,
            out_shape=field,
            input_output_aliases={0: 0},
            scratch_shapes=[wide],
            compiler_params=params(2),
            cost_estimate=pl.CostEstimate(
                flops=size * matmul // 2, bytes_accessed=3 * size * field_bytes, transcendentals=0
            ),
            name="finish_%d" % members[0],
        )(base, received, pick, spread)
    last = back_groups[-1][0]
    return pl.pallas_call(
        last_finish_kernel,
        grid=(mom_local // pair,),
        in_specs=[pair_at(last), plain_block, whole(square), whole(square)],
        out_specs=pair_at(last),
        out_shape=field,
        input_output_aliases={0: 0},
        compiler_params=params(1),
        cost_estimate=pl.CostEstimate(flops=matmul // 2, bytes_accessed=3 * field_bytes, transcendentals=0),
        name="finish_last",
    )(base, finished[-1], pick, spread)


def solution(mesh):
    in_specs = (P(None, AXES, None, None), P(None, AXES, None, None), P(), P(), P(), P(), P())
    return jax.shard_map(
        per_device, mesh=mesh, in_specs=in_specs, out_specs=P(None, AXES, None, None), check_vma=False
    )
```

profile of v0, /device:TPU:15, one launch (start us, length us, event | category | flops | bytes accessed | tf_op | source)
XLA Modules:
  0.0 625.6 jit_solution(10003250402630697154)
XLA Ops:
  0.0 0.7 slice_add_fusion
  0.7 0.8 fusion.12
  1.4 10.3 %product_first.1 = (bf16[3,8,512,512]{3,2,1,0:T(8,128)(2,1)}, bf16[32,1,8,2,8,512]{5,4,3,2,1,0:T(8,128)(2,1)}, f32[8,128]{1,0:T(8,128)}) custom-call(bf16[3,8,512,512]{3,2,1,0:T(8,128)(2,1)} %vertex_ref.3, bf16[3,8,512,512]{3,2,1,0:T(8,128)(2,1)} %loop_ref.3, bf16[256,256]{1,0:T(8,128)(2,1)} %get-tuple-element.29.pick_ref, ...), custom_call_target="tpu_custom_call" | custom-call | flops 5368709120 | bytes 16777216 | tf_op jit(solution)/shard_map/product_first/pallas_call | solution.py:233
  11.8 6.3 %all-to-all-start = ((bf16[32,1,8,2,8,512]{5,4,3,2,1,0:T(8,128)(2,1)}), bf16[32,1,8,2,8,512]{5,4,3,2,1,0:T(8,128)(2,1)}, u32[]{:S(2)}, u32[]{:S(2)}) async-start(bf16[32,1,8,2,8,512]{5,4,3,2,1,0:T(8,128)(2,1)} %get-tuple-element.21), calls=%async_computation | async-start | bytes 8388608 | tf_op jit(solution)/shard_map/all_to_all | solution.py:224
  18.1 25.3 %product_1.1 = (bf16[3,8,512,512]{3,2,1,0:T(8,128)(2,1)}, bf16[32,2,2,8,8,512]{5,4,3,2,1,0:T(8,128)(2,1)}, f32[8,128]{1,0:T(8,128)}) custom-call(bf16[3,8,512,512]{3,2,1,0:T(8,128)(2,1)} %vertex_ref.3, bf16[3,8,512,512]{3,2,1,0:T(8,128)(2,1)} %loop_ref.3, bf16[256,256]{1,0:T(8,128)(2,1)} %get-tuple-element.29.pick_ref, ...), custom_call_target="tpu_custom_call", output_to_operand_aliasing={{0}: (4, {})} | custom-call | flops 10737418240 | bytes 33554432 | tf_op jit(solution)/shard_map/product_1/pallas_call | solution.py:248
  43.4 68.0 %all-to-all-done = bf16[32,1,8,2,8,512]{5,4,3,2,1,0:T(8,128)(2,1)} async-done(((bf16[32,1,8,2,8,512]{5,4,3,2,1,0:T(8,128)(2,1)}), bf16[32,1,8,2,8,512]{5,4,3,2,1,0:T(8,128)(2,1)}, u32[]{:S(2)}, u32[]{:S(2)}) %all-to-all-start) | async-done | bytes 4194336 | tf_op jit(solution)/shard_map/all_to_all | solution.py:224
  111.4 0.0 copy-start.1
  111.4 0.0 copy-start.4
  111.4 0.0 copy-start
  111.4 0.0 slice-start
  111.4 0.0 copy-start.2
  111.4 0.0 copy-start.3
  111.4 6.9 %all-to-all-start.1 = ((bf16[32,2,2,8,8,512]{5,4,3,2,1,0:T(8,128)(2,1)}), bf16[32,2,2,8,8,512]{5,4,3,2,1,0:T(8,128)(2,1)}, u32[]{:S(2)}, u32[]{:S(2)}) async-start(bf16[32,2,2,8,8,512]{5,4,3,2,1,0:T(8,128)(2,1)} %get-tuple-element.22), calls=%async_computation.1 | async-start | bytes 16777216 | tf_op jit(solution)/shard_map/all_to_all | solution.py:224
  118.3 0.0 copy-done.1
  118.3 0.0 copy-done.4
  118.4 0.0 copy-done
  118.4 1.9 gather_fusion
  120.3 0.0 slice-done
  120.4 0.1 constant_dynamic-slice_fusion
  120.5 0.8 fusion.19.cycle_ref
  121.2 0.0 copy-done.2
  121.2 0.0 copy-done.3
  121.2 0.5 broadcast_multiply_fusion
  121.8 0.7 broadcast_add_fusion.reach_ref
  122.5 4.2 add_convert_fusion
  126.6 8.9 %copy.22 = bf16[32,1,8,2,8,512]{5,2,4,3,1,0:T(8,128)(2,1)} copy(bf16[32,1,8,2,8,512]{5,4,3,2,1,0:T(8,128)(2,1)} %all-to-all-done) | data formatting | bytes 8388608 | tf_op jit(solution)/shard_map/layout_constraint | solution.py:243
  135.6 170.0 %all-to-all-done.1.refs_1_ = bf16[32,2,2,8,8,512]{5,4,3,2,1,0:T(8,128)(2,1)} async-done(((bf16[32,2,2,8,8,512]{5,4,3,2,1,0:T(8,128)(2,1)}), bf16[32,2,2,8,8,512]{5,4,3,2,1,0:T(8,128)(2,1)}, u32[]{:S(2)}, u32[]{:S(2)}) %all-to-all-start.1) | async-done | bytes 8388640 | tf_op jit(solution)/shard_map/all_to_all | solution.py:224
  305.5 18.8 %lattice_0.1.refs_2_ = bf16[32,2,2,8,8,512]{5,4,3,2,1,0:T(8,128)(2,1)} custom-call(f32[3,3]{1,0:T(4,128)} %get-tuple-element.32.own_ref, f32[3,3]{1,0:T(4,128)} %get-tuple-element.31.cross_ref, bf16[256,256]{1,0:T(8,128)(2,1)} %get-tuple-element.25.plus_ref, bf16[256,256]{1,0:T(8,128)(2,1)} %get-tuple-element.24.minus_ref, ...), custom_call_target="tpu_custom_call" | custom-call | flops 8589934592 | bytes 20971520 | tf_op jit(solution)/shard_map/lattice_0/pallas_call | solution.py:289
  324.4 6.9 %all-to-all-start.2 = ((bf16[32,2,2,8,8,512]{5,4,3,2,1,0:T(8,128)(2,1)}), bf16[32,2,2,8,8,512]{5,4,3,2,1,0:T(8,128)(2,1)}, u32[]{:S(2)}, u32[]{:S(2)}) async-start(bf16[32,2,2,8,8,512]{5,4,3,2,1,0:T(8,128)(2,1)} %lattice_0.1.refs_2_), calls=%async_computation.2 | async-start | bytes 16777216 | tf_op jit(solution)/shard_map/all_to_all | solution.py:224
  331.3 14.1 %lattice_2.1 = bf16[32,1,2,8,8,512]{5,4,3,2,1,0:T(8,128)(2,1)} custom-call(f32[3,3]{1,0:T(4,128)} %get-tuple-element.32.own_ref, f32[3,3]{1,0:T(4,128)} %get-tuple-element.31.cross_ref, bf16[256,256]{1,0:T(8,128)(2,1)} %get-tuple-element.25.plus_ref, bf16[256,256]{1,0:T(8,128)(2,1)} %get-tuple-element.24.minus_ref, ...), custom_call_target="tpu_custom_call" | custom-call | flops 7516192768 | bytes 16777216 | tf_op jit(solution)/shard_map/lattice_2/pallas_call | solution.py:289
  345.4 6.0 copy.21
  351.4 167.1 %all-to-all-done.2.received_ref = bf16[32,2,2,8,8,512]{5,4,3,2,1,0:T(8,128)(2,1)} async-done(((bf16[32,2,2,8,8,512]{5,4,3,2,1,0:T(8,128)(2,1)}), bf16[32,2,2,8,8,512]{5,4,3,2,1,0:T(8,128)(2,1)}, u32[]{:S(2)}, u32[]{:S(2)}) %all-to-all-start.2) | async-done | bytes 8388640 | tf_op jit(solution)/shard_map/all_to_all | solution.py:224
  518.5 6.9 %all-to-all-start.3 = ((bf16[32,1,8,2,8,512]{5,4,3,2,1,0:T(8,128)(2,1)}), bf16[32,1,8,2,8,512]{5,4,3,2,1,0:T(8,128)(2,1)}, u32[]{:S(2)}, u32[]{:S(2)}) async-start(bf16[32,1,8,2,8,512]{5,4,3,2,1,0:T(8,128)(2,1)} %bitcast.6), calls=%async_computation.3 | async-start | bytes 8388608 | tf_op jit(solution)/shard_map/all_to_all | solution.py:224
  525.4 19.6 %finish_0.1.base_ref = bf16[3,8,512,512]{3,2,1,0:T(8,128)(2,1)} custom-call(bf16[3,8,512,512]{3,2,1,0:T(8,128)(2,1)} %get-tuple-element.15.base_ref, bf16[32,2,2,8,8,512]{5,4,3,2,1,0:T(8,128)(2,1)} %all-to-all-done.2.received_ref, bf16[256,256]{1,0:T(8,128)(2,1)} %get-tuple-element.29.pick_ref, ...), custom_call_target="tpu_custom_call", output_to_operand_aliasing={{}: (0, {})} | custom-call | flops 2147483648 | bytes 25165824 | tf_op jit(solution)/shard_map/finish_0/pallas_call | solution.py:321
  545.0 73.7 %all-to-all-done.3.received_ref = bf16[32,1,8,2,8,512]{5,4,3,2,1,0:T(8,128)(2,1)} async-done(((bf16[32,1,8,2,8,512]{5,4,3,2,1,0:T(8,128)(2,1)}), bf16[32,1,8,2,8,512]{5,4,3,2,1,0:T(8,128)(2,1)}, u32[]{:S(2)}, u32[]{:S(2)}) %all-to-all-start.3) | async-done | bytes 4194336 | tf_op jit(solution)/shard_map/all_to_all | solution.py:224
  618.7 6.9 %finish_last.1 = bf16[3,8,512,512]{3,2,1,0:T(8,128)(2,1)} custom-call(bf16[3,8,512,512]{3,2,1,0:T(8,128)(2,1)} %finish_0.1.base_ref, bf16[32,1,8,2,8,512]{5,4,3,2,1,0:T(8,128)(2,1)} %all-to-all-done.3.received_ref, bf16[256,256]{1,0:T(8,128)(2,1)} %get-tuple-element.29.pick_ref, ...), custom_call_target="tpu_custom_call", output_to_operand_aliasing={{}: (0, {})} | custom-call | flops 1073741824 | bytes 12582912 | tf_op jit(solution)/shard_map/finish_last/pallas_call | solution.py:336
  (6 shorter events, 0.0 us)
Async XLA Ops:
  11.8 99.6 %all-to-all-start = ((bf16[32,1,8,2,8,512]{5,4,3,2,1,0:T(8,128)(2,1)}), bf16[32,1,8,2,8,512]{5,4,3,2,1,0:T(8,128)(2,1)}, u32[]{:S(2)}, u32[]{:S(2)}) async-start(bf16[32,1,8,2,8,512]{5,4,3,2,1,0:T(8,128)(2,1)} %get-tuple-element.21), calls=%async_computation | async-start | bytes 8388608 | tf_op jit(solution)/shard_map/all_to_all | solution.py:224
  111.4 6.9 %copy-start.1 = (s32[512]{0:T(512)S(1)}, s32[512]{0:T(512)}, u32[]{:S(2)}) copy-start(s32[512]{0:T(512)} %param.12) | copy-start | bytes 6148
  111.4 6.9 %copy-start.4 = (s32[256]{0:T(256)S(1)}, s32[256]{0:T(256)}, u32[]{:S(2)}) copy-start(s32[256]{0:T(256)} %param.13) | copy-start | bytes 3076
  111.4 7.0 %copy-start = (s32[512]{0:T(512)S(1)}, s32[512]{0:T(512)}, u32[]{:S(2)}) copy-start(s32[512]{0:T(512)} %param.11) | copy-start | bytes 6148
  111.4 9.0 %slice-start = ((s32[512]{0:T(512)}), s32[256]{0:T(256)S(1)}, s32[]{:S(2)}) async-start(s32[512]{0:T(512)} %param.11), calls=%async_computation.4 | async-start | bytes 2048 | tf_op jit(solution)/shard_map/slice | solution.py:272
  111.4 9.9 %copy-start.2 = (f32[3,3]{1,0:T(4,128)S(1)}, f32[3,3]{1,0:T(4,128)}, u32[]{:S(2)}) copy-start(f32[3,3]{1,0:T(4,128)} %param.10) | copy-start | bytes 112
  111.4 9.8 %copy-start.3 = (f32[3,3]{1,0:T(4,128)S(1)}, f32[3,3]{1,0:T(4,128)}, u32[]{:S(2)}) copy-start(f32[3,3]{1,0:T(4,128)} %param.9) | copy-start | bytes 112
  111.4 194.1 %all-to-all-start.1 = ((bf16[32,2,2,8,8,512]{5,4,3,2,1,0:T(8,128)(2,1)}), bf16[32,2,2,8,8,512]{5,4,3,2,1,0:T(8,128)(2,1)}, u32[]{:S(2)}, u32[]{:S(2)}) async-start(bf16[32,2,2,8,8,512]{5,4,3,2,1,0:T(8,128)(2,1)} %get-tuple-element.22), calls=%async_computation.1 | async-start | bytes 16777216 | tf_op jit(solution)/shard_map/all_to_all | solution.py:224
  324.4 194.1 %all-to-all-start.2 = ((bf16[32,2,2,8,8,512]{5,4,3,2,1,0:T(8,128)(2,1)}), bf16[32,2,2,8,8,512]{5,4,3,2,1,0:T(8,128)(2,1)}, u32[]{:S(2)}, u32[]{:S(2)}) async-start(bf16[32,2,2,8,8,512]{5,4,3,2,1,0:T(8,128)(2,1)} %lattice_0.1.refs_2_), calls=%async_computation.2 | async-start | bytes 16777216 | tf_op jit(solution)/shard_map/all_to_all | solution.py:224
  518.5 100.2 %all-to-all-start.3 = ((bf16[32,1,8,2,8,512]{5,4,3,2,1,0:T(8,128)(2,1)}), bf16[32,1,8,2,8,512]{5,4,3,2,1,0:T(8,128)(2,1)}, u32[]{:S(2)}, u32[]{:S(2)}) async-start(bf16[32,1,8,2,8,512]{5,4,3,2,1,0:T(8,128)(2,1)} %bitcast.6), calls=%async_computation.3 | async-start | bytes 8388608 | tf_op jit(solution)/shard_map/all_to_all | solution.py:224
where the time goes:
time: 629 us; the launch traced here: 626 us
  waiting for transfers between devices  479 us (76%)
  Pallas kernels  95.1 us (15%)
  starting transfers between devices  26.9 us (4%)
  local copies, waits for them, and re-layouts  17 us (3%)
  other arithmetic  7.65 us (1%)
    all_to_all x4, waiting for transfers between devices, exchange(): lax.all_to_all(outgoing, AXES, split_axis=0, concat_axis=0, tiled=True)  479 us
    pallas_call x2, Pallas kernels, per_device(): pl.pallas_call(functools.partial(lattice_kernel, sizes, members), grid=(g...  33 us
    all_to_all x4, starting transfers between devices, exchange(): lax.all_to_all(outgoing, AXES, split_axis=0, concat_axis=0, tiled=True)  26.9 us
    pallas_call x1, Pallas kernels, per_device(): pl.pallas_call(functools.partial(product_kernel, mom_local, places), grid...  25.3 us
    pallas_call x1, Pallas kernels, per_device(): pl.pallas_call(functools.partial(finish_kernel, mom_local), grid=(size, m...  19.6 us
  transfers between devices with their start and end apart: 4, of which 4 were waited for; matrix products, arithmetic and copies ran while one was open for 4% of the time, Pallas kernels for 9%

commit v1 on v0

--- a/solution.py
+++ b/solution.py
@@ -3,6 +3,7 @@
 
 import jax
 import jax.numpy as jnp
+import numpy as np
 from jax import lax
 from jax.experimental import pallas as pl
 from jax.experimental.layout import Layout, with_layout_constraint
@@ -186,7 +187,7 @@
     return pltpu.CompilerParams(dimension_semantics=("arbitrary",) * axes, vmem_limit_bytes=VMEM_LIMIT)
 
 
-def per_device(vertex, loop_matrix, own_mix, cross_mix, shells, partner, grid_index):
+def general_flow(vertex, loop_matrix, own_mix, cross_mix, shells, partner, grid_index):
     places = lax.axis_size("mom") * lax.axis_size("bond")
     place = lax.axis_index("mom") * lax.axis_size("bond") + lax.axis_index("bond")
     channels, mom_local, bonds, _ = vertex.shape
@@ -346,6 +347,486 @@
     )(base, finished[-1], pick, spread)
 
 
+MESH = pl.DeviceIdType.MESH
+
+
+def flow_kernel(
+    parts,
+    vertex_ref,
+    loop_ref,
+    own_ref,
+    cross_ref,
+    partner_ref,
+    shells_ref,
+    grid_ref,
+    base_ref,
+    back_ref,
+    send_ref,
+    recv_ref,
+    wide_ref,
+    vertex_buf,
+    loop_buf,
+    base_buf,
+    tile_buf,
+    pick_ref,
+    spread_ref,
+    block_ref,
+    plus_ref,
+    minus_ref,
+    turn_ref,
+    cycle_ref,
+    row_ref,
+    col_ref,
+    load_sem,
+    store_sem,
+    self_sem,
+    out_sem,
+    in_sem,
+    home_sem,
+    finish_sem,
+):
+    bf16, f32 = jnp.bfloat16, jnp.float32
+    chunks, channels, places, depth, width = send_ref.shape
+    mom_local, bonds = vertex_ref.shape[1], vertex_ref.shape[-1]
+    half, count = bonds // 2, places * mom_local
+    group = half // places
+    pair = 2 * group
+    side = math.isqrt(count)
+    steps = channels * mom_local
+    columns = lax.axis_size("bond")
+    place = lax.axis_index("mom") * columns + lax.axis_index("bond")
+
+    def device(offset):
+        at = lax.rem(place + offset, places)
+        return at, (lax.div(at, columns), lax.rem(at, columns))
+
+    barrier = pltpu.get_barrier_semaphore()
+
+    def greet(offset, carry):
+        pl.semaphore_signal(barrier, inc=1, device_id=device(offset)[1], device_id_type=MESH)
+        return carry
+
+    lax.fori_loop(1, places, greet, 0)
+
+    def loads(step, slot):
+        c, n = lax.div(step, mom_local), lax.rem(step, mom_local)
+        return [
+            pltpu.make_async_copy(source.at[c, n], target.at[slot], load_sem.at[k, slot])
+            for k, (source, target) in enumerate(((vertex_ref, vertex_buf), (loop_ref, loop_buf)))
+        ]
+
+    def store(step, slot):
+        c, n = lax.div(step, mom_local), lax.rem(step, mom_local)
+        return pltpu.make_async_copy(base_buf.at[slot], base_ref.at[c, n], store_sem.at[slot])
+
+    for copy in loads(0, 0):
+        copy.start()
+
+    down = lax.broadcasted_iota(jnp.int32, (half, half), 0)
+    lower_partner = partner_ref[:, :half] - half
+    pick_ref[...] = jnp.where(down == partner_ref[:, half:], 1.0, 0.0).astype(bf16)
+    spread_ref[...] = jnp.where(down == lower_partner, 1.0, 0.0).astype(bf16)
+
+    def forward(unit_k, unit_c, first, size):
+        unit = unit_k * channels + unit_c
+
+        def one(offset, carry):
+            at, target = device(offset)
+            rows = pl.ds(first, size)
+            pltpu.make_async_remote_copy(
+                src_ref=send_ref.at[unit_k, unit_c, at, rows],
+                dst_ref=recv_ref.at[unit_k, unit_c, place, rows],
+                send_sem=out_sem.at[0, unit],
+                recv_sem=in_sem.at[0, unit],
+                device_id=target,
+                device_id_type=MESH,
+            ).start()
+            return carry
+
+        lax.fori_loop(1, places, one, 0)
+
+    def backward(unit_k, unit_c):
+        unit = unit_k * channels + unit_c
+
+        def one(offset, carry):
+            at, target = device(offset)
+            pltpu.make_async_remote_copy(
+                src_ref=send_ref.at[unit_k, unit_c, at],
+                dst_ref=back_ref.at[unit_k, unit_c, place],
+                send_sem=out_sem.at[1, unit],
+                recv_sem=in_sem.at[1, unit],
+                device_id=target,
+                device_id_type=MESH,
+            ).start()
+            return carry
+
+        lax.fori_loop(1, places, one, 0)
+
+    def all_of(way, unit_k, unit_c):
+        unit = unit_k * channels + unit_c
+        landing = back_ref if way else recv_ref
+        return pltpu.make_async_remote_copy(
+            src_ref=send_ref.at[unit_k, unit_c, pl.ds(0, places - 1)],
+            dst_ref=landing.at[unit_k, unit_c, pl.ds(0, places - 1)],
+            send_sem=out_sem.at[way, unit],
+            recv_sem=in_sem.at[way, unit],
+            device_id=device(1)[1],
+            device_id_type=MESH,
+        )
+
+    def own_block(way, unit_k, unit_c):
+        unit = unit_k * channels + unit_c
+        landing, sem = (back_ref, home_sem) if way else (recv_ref, self_sem)
+        return pltpu.make_async_copy(
+            send_ref.at[unit_k, unit_c, place], landing.at[unit_k, unit_c, place], sem.at[unit]
+        )
+
+    part = mom_local // parts
+
+    def product_step(step, carry):
+        slot = lax.rem(step, 2)
+        c, n = lax.div(step, mom_local), lax.rem(step, mom_local)
+
+        @pl.when(step + 1 < steps)
+        def _():
+            for copy in loads(step + 1, 1 - slot):
+                copy.start()
+
+        for copy in loads(step, slot):
+            copy.wait()
+        vertex = vertex_buf[slot]
+        half_product = dot(vertex, loop_buf[slot]).astype(bf16)
+        product = dot(half_product, vertex)
+        rounded = product.astype(bf16)
+        left = rounded[:, :half]
+        right = dot(rounded[:, half:], spread_ref[...]).astype(bf16)
+        rows = pl.ds(pl.multiple_of(n * pair, pair), pair)
+        for at, piece in enumerate((left, right)):
+            upper = dot(pick_ref[...], piece[half:])
+            lower = piece[:half].astype(f32)
+            for k in range(chunks):
+                cols = slice(k * LANES, (k + 1) * LANES)
+                both = jnp.concatenate(
+                    [lower[:, cols].reshape(places, group, LANES), upper[:, cols].reshape(places, group, LANES)], axis=1
+                )
+                send_ref[k, c, :, rows, at * LANES : (at + 1) * LANES] = both.astype(bf16)
+
+        @pl.when(step >= 2)
+        def _():
+            store(step - 2, slot).wait()
+
+        base_buf[slot] = (product + vertex.astype(f32)).astype(bf16)
+        store(step, slot).start()
+
+        @pl.when(step == part - 1)
+        def _():
+            pl.semaphore_wait(barrier, places - 1)
+
+        @pl.when((c == 0) & (lax.rem(n, part) == part - 1))
+        def _():
+            forward(0, 0, pl.multiple_of((n - part + 1) * pair, part * pair), part * pair)
+
+        @pl.when((c > 0) & (n == mom_local - 1))
+        def _():
+            forward(0, c, 0, depth)
+
+        return carry
+
+    lax.fori_loop(0, steps, product_step, 0)
+
+    def later_chunk(unit, carry):
+        forward(lax.div(unit, channels), lax.rem(unit, channels), 0, depth)
+        return carry
+
+    lax.fori_loop(channels, chunks * channels, later_chunk, 0)
+
+    def start_own(unit, carry):
+        own_block(0, lax.div(unit, channels), lax.rem(unit, channels)).start()
+        return carry
+
+    lax.fori_loop(0, chunks * channels, start_own, 0)
+    for step in (steps - 2, steps - 1):
+        store(step, step % 2).wait()
+
+    def floor_div(value, by):
+        return jnp.floor((value + 0.5) * (1.0 / by))
+
+    points = lax.broadcasted_iota(jnp.int32, (count, count), 0).astype(f32)
+    disp_x = floor_div(points, side)
+    disp_y = points - side * disp_x
+    far = []
+    for disp in (disp_x, disp_y):
+        moved = disp + side // 2
+        far.append(jnp.abs(moved - side * floor_div(moved, side) - side // 2))
+    cycle_ref[...] = jnp.maximum(far[0], far[1])
+    grid = grid_ref[...].astype(f32)
+    wave_x = floor_div(grid, side)
+    wave_y = grid - side * wave_x
+    phases = disp_x * wave_x + disp_y * wave_y
+    phases = phases - side * floor_div(phases, side)
+    angles = np.arange(side, dtype=np.float32) * np.float32(2.0 * math.pi / side)
+    cas = (np.cos(angles) + np.sin(angles)).astype(np.float32)
+    plus = jnp.zeros_like(phases)
+    minus = jnp.zeros_like(phases)
+    for phase in range(side):
+        here = phases == float(phase)
+        plus = jnp.where(here, float(cas[phase]), plus)
+        minus = jnp.where(here, float(cas[(side - phase) % side]), minus)
+    plus_ref[...] = plus.astype(bf16)
+    minus_ref[...] = minus.astype(bf16)
+    turn_ref[...] = plus.T.astype(bf16)
+
+    shells = shells_ref[...].astype(f32)
+    low_shells = shells[:, :half]
+    up_shells = dot(jnp.broadcast_to(shells[:, half:], (8, half)).astype(bf16), spread_ref[...])[:1]
+    lane = lax.broadcasted_iota(jnp.int32, (group, half), 1)
+    mine = lane == place * group + lax.broadcasted_iota(jnp.int32, (group, half), 0)
+    for s, line in enumerate((low_shells, up_shells)):
+        column = jnp.sum(jnp.where(mine, jnp.broadcast_to(line, (group, half)), 0.0), axis=1, keepdims=True)
+        row_ref[s * group : (s + 1) * group] = jnp.broadcast_to(column, (group, width))
+        for k in range(chunks):
+            cols = slice(k * LANES, (k + 1) * LANES)
+            col_ref[k, :, s * LANES : (s + 1) * LANES] = jnp.broadcast_to(line[:, cols], (8, LANES))
+    for k in range(chunks):
+        cols = slice(k * LANES, (k + 1) * LANES)
+        block_ref[k] = pick_ref[cols, cols]
+
+    def lattice_chunk(k, carry):
+        for c in range(channels):
+            all_of(0, k, c).wait_recv()
+            own_block(0, k, c).wait()
+
+        def widen(at, carry):
+            for c in range(channels):
+                rows = pl.ds(pl.multiple_of(at * depth, depth), depth)
+                block = recv_ref[k, c, at].astype(f32)
+                for t in range(2):
+                    wide_ref[c, t, rows] = block[:, t * LANES : (t + 1) * LANES]
+            return carry
+
+        lax.fori_loop(0, places, widen, 0)
+
+        def row_step(i, carry):
+            def lines(s):
+                return pl.ds(s * group + i, count, stride=pair)
+
+            blocks = [
+                [
+                    jnp.concatenate([wide_ref[c, t, lines(s)] for t in range(2)], axis=1).astype(bf16)
+                    for s in range(2)
+                ]
+                for c in range(channels)
+            ]
+            for s in range(2):
+                mixed = [None] * channels
+                for c in range(channels):
+                    own = dot(plus_ref[...], blocks[c][s])
+                    crossed = dot(minus_ref[...], blocks[c][1 - s])
+                    crossed = jnp.concatenate([crossed[:, LANES:], crossed[:, :LANES]], axis=1)
+                    for d in range(channels):
+                        term = own_ref[d, c] * own + cross_ref[d, c] * crossed
+                        mixed[d] = term if c == 0 else mixed[d] + term
+                reach = row_ref[pl.ds(s * group + i, 1)] + col_ref[k, :1]
+                kept = cycle_ref[:, :width] <= reach
+                for d in range(channels):
+                    projected = jnp.where(kept, mixed[d] * (1.0 / count), 0.0).astype(bf16)
+                    returned = dot(turn_ref[...], projected)
+                    for t in range(2):
+                        wide_ref[d, t, lines(s)] = returned[:, t * LANES : (t + 1) * LANES]
+            return carry
+
+        lax.fori_loop(0, group, row_step, 0)
+        for c in range(channels):
+            all_of(0, k, c).wait_send()
+
+        def narrow(at, carry):
+            for d in range(channels):
+                rows = pl.ds(pl.multiple_of(at * depth, depth), depth)
+                block = jnp.concatenate([wide_ref[d, t, rows] for t in range(2)], axis=1)
+                send_ref[k, d, at] = block.astype(bf16)
+            return carry
+
+        lax.fori_loop(0, places, narrow, 0)
+        for d in range(channels):
+            backward(k, d)
+        for d in range(channels):
+            own_block(1, k, d).start()
+        return carry
+
+    lax.fori_loop(0, chunks, lattice_chunk, 0)
+
+    def finish_unit(unit, carry):
+        k, d = lax.div(unit, channels), lax.rem(unit, channels)
+        all_of(1, k, d).wait_recv()
+        own_block(1, k, d).wait()
+        tiles = [
+            base_ref.at[d, :, :, pl.ds(pl.multiple_of(k * LANES + t * half, LANES), LANES)] for t in range(2)
+        ]
+        arrivals = [pltpu.make_async_copy(back_ref.at[k, d], recv_ref.at[0, 0], finish_sem.at[2])] + [
+            pltpu.make_async_copy(tiles[t], tile_buf.at[t], finish_sem.at[t]) for t in range(2)
+        ]
+        for copy in arrivals:
+            copy.start()
+        for copy in arrivals:
+            copy.wait()
+
+        def finish_matrix(n, carry):
+            rows = pl.ds(pl.multiple_of(n * pair, pair), pair)
+            block = recv_ref[0, 0, :, rows].astype(f32)
+            for s in range(2):
+                there = slice(s * half, (s + 1) * half)
+                piece = block[:, s * group : (s + 1) * group].reshape(half, width)
+                if s:
+                    piece = dot(spread_ref[...], piece.astype(bf16))
+                right = dot(piece[:, LANES:].astype(bf16), block_ref[k])
+                for t, add in enumerate((piece[:, :LANES], right)):
+                    tile_buf[t, n, there] = (tile_buf[t, n, there].astype(f32) + add).astype(bf16)
+            return carry
+
+        lax.fori_loop(0, mom_local, finish_matrix, 0)
+        departures = [pltpu.make_async_copy(tile_buf.at[t], tiles[t], finish_sem.at[t]) for t in range(2)]
+        for copy in departures:
+            copy.start()
+        for copy in departures:
+            copy.wait()
+        return carry
+
+    units = chunks * channels
+    lax.fori_loop(0, units - 1, finish_unit, 0)
+    all_of(1, chunks - 1, channels - 1).wait_recv()
+    own_block(1, chunks - 1, channels - 1).wait()
+
+    def drain(unit, carry):
+        all_of(1, lax.div(unit, channels), lax.rem(unit, channels)).wait_send()
+        return carry
+
+    lax.fori_loop(0, units, drain, 0)
+
+
+def tile_finish_kernel(base_ref, received_ref, spread_ref, block_ref, out_ref):
+    places, depth = received_ref.shape[2:4]
+    batch, bonds = base_ref.shape[1:3]
+    half = bonds // 2
+    group = half // places
+    pair = 2 * group
+
+    def put(right):
+        for n in range(batch):
+            block = received_ref[0, 0, :, n * pair : (n + 1) * pair].astype(jnp.float32)
+            for s in range(2):
+                there = slice(s * half, (s + 1) * half)
+                piece = block[:, s * group : (s + 1) * group].reshape(half, LANES)
+                if s:
+                    piece = dot(spread_ref[...], piece.astype(jnp.bfloat16))
+                if right:
+                    piece = dot(piece.astype(jnp.bfloat16), block_ref[...])
+                out_ref[0, n, there] = (base_ref[0, n, there].astype(jnp.float32) + piece).astype(jnp.bfloat16)
+
+    @pl.when(pl.program_id(0) == 0)
+    def _():
+        put(False)
+
+    @pl.when(pl.program_id(0) == 1)
+    def _():
+        put(True)
+
+
+def chunked_flow(vertex, loop_matrix, own_mix, cross_mix, shells, partner, grid_index):
+    places = lax.axis_size("mom") * lax.axis_size("bond")
+    channels, mom_local, bonds, _ = vertex.shape
+    count = grid_index.shape[0]
+    half = bonds // 2
+    group = half // places
+    chunks = half // LANES
+    width = 2 * LANES
+    depth = mom_local * 2 * group
+    units = chunks * channels
+    bf16, f32 = jnp.bfloat16, jnp.float32
+    parts = mom_local // PAIR if mom_local % PAIR == 0 else 1
+    anywhere = pl.BlockSpec(memory_space=pl.ANY)
+    scalars = pl.BlockSpec(memory_space=pltpu.SMEM)
+    inside = pl.BlockSpec(memory_space=pltpu.VMEM)
+    dma = pltpu.SemaphoreType.DMA
+    base, back = pl.pallas_call(
+        functools.partial(flow_kernel, parts),
+        in_specs=[anywhere, anywhere, scalars, scalars, inside, inside, inside],
+        out_specs=[anywhere, anywhere],
+        out_shape=[
+            jax.ShapeDtypeStruct(vertex.shape, bf16),
+            jax.ShapeDtypeStruct((chunks, channels, places, depth, width), bf16),
+        ],
+        scratch_shapes=[
+            pltpu.VMEM((chunks, channels, places, depth, width), bf16),
+            pltpu.VMEM((chunks, channels, places, depth, width), bf16),
+            pltpu.VMEM((channels, 2, places * depth, LANES), f32),
+            pltpu.VMEM((2, bonds, bonds), bf16),
+            pltpu.VMEM((2, bonds, bonds), bf16),
+            pltpu.VMEM((2, bonds, bonds), bf16),
+            pltpu.VMEM((2, mom_local, bonds, LANES), bf16),
+            pltpu.VMEM((half, half), bf16),
+            pltpu.VMEM((half, half), bf16),
+            pltpu.VMEM((chunks, LANES, LANES), bf16),
+            pltpu.VMEM((count, count), bf16),
+            pltpu.VMEM((count, count), bf16),
+            pltpu.VMEM((count, count), bf16),
+            pltpu.VMEM((count, count), f32),
+            pltpu.VMEM((2 * group, width), f32),
+            pltpu.VMEM((chunks, 8, width), f32),
+            dma((2, 2)),
+            dma((2,)),
+            dma((units,)),
+            dma((2, units)),
+            dma((2, units)),
+            dma((units,)),
+            dma((3,)),
+        ],
+        compiler_params=pltpu.CompilerParams(collective_id=0, has_side_effects=True, vmem_limit_bytes=VMEM_LIMIT),
+        name="flow",
+    )(
+        vertex,
+        loop_matrix,
+        own_mix,
+        cross_mix,
+        partner.reshape(1, bonds),
+        shells.reshape(1, bonds),
+        grid_index.reshape(1, count),
+    )
+
+    lower_partner = partner[:half] - half
+    uppers = jnp.arange(half, dtype=jnp.int32)
+    spread = (lower_partner[None, :] == uppers[:, None]).astype(bf16)
+    edge = (chunks - 1) * LANES
+    block = (lower_partner[edge:, None] - edge == uppers[None, :LANES]).astype(bf16)
+    batch = math.gcd(mom_local, 4)
+    tile = pl.BlockSpec((1, batch, bonds, LANES), lambda t, i: (channels - 1, i, 0, chunks - 1 + t * chunks))
+    return pl.pallas_call(
+        tile_finish_kernel,
+        grid=(2, mom_local // batch),
+        in_specs=[
+            tile,
+            pl.BlockSpec(
+                (1, 1, places, batch * 2 * group, LANES), lambda t, i: (chunks - 1, channels - 1, 0, i, t)
+            ),
+            whole((half, half)),
+            whole((LANES, LANES)),
+        ],
+        out_specs=tile,
+        out_shape=jax.ShapeDtypeStruct(vertex.shape, bf16),
+        input_output_aliases={0: 0},
+        compiler_params=params(2),
+        name="finish_tile",
+    )(base, back, spread, block)
+
+
+def per_device(vertex, *others):
+    places = lax.axis_size("mom") * lax.axis_size("bond")
+    half = vertex.shape[-1] // 2
+    group = half // places
+    if group and group % 8 == 0 and half % LANES == 0 and places * vertex.shape[1] >= 2 * LANES:
+        return chunked_flow(vertex, *others)
+    return general_flow(vertex, *others)
+
+
 def solution(mesh):
     in_specs = (P(None, AXES, None, None), P(None, AXES, None, None), P(), P(), P(), P(), P())
     return jax.shard_map(

time: 629 us -> 567 us (0.901)
  waiting for transfers between devices: 479 us -> 0 us
  Pallas kernels: 95.1 us -> 553 us
  starting transfers between devices: 26.9 us -> 0 us
  local copies, waits for them, and re-layouts: 17 us -> 10.4 us
    all_to_all x4 -> x0, waiting for transfers between devices: 479 us -> none  [exchange(): lax.all_to_all(outgoing, AXES, split_axis=0, concat_axis=0, tiled=True)]
    pallas_call x6 -> x2, Pallas kernels: 95.1 us -> 553 us  [the longest x1 548 us: chunked_flow(): pl.pallas_call(functools.partial(flow_kernel, parts), in_specs=[anywhere,...]
    all_to_all x4 -> x0, starting transfers between devices: 26.9 us -> none  [exchange(): lax.all_to_all(outgoing, AXES, split_axis=0, concat_axis=0, tiled=True)]
    unnamed x10 -> x1, local copies, waits for them, and re-layouts: 0.02 us -> 10.4 us
    another operation x1 -> x0, local copies, waits for them, and re-layouts: 8.92 us -> none  [per_device(): with_layout_constraint(exchange(outgoing), Layout(major_to_minor=tuple(ra...]
  transfers between devices with their start and end apart: 4 -> 0, of which waited for: 4 -> 0; matrix products, arithmetic and copies ran while one was open for 4% -> 0% of each run, Pallas kernels for 9% -> 0%
where the time goes in v1:
time: 567 us; the launch traced here: 566 us
  Pallas kernels  553 us (98%)
  local copies, waits for them, and re-layouts  10.4 us (2%)
    pallas_call x1, Pallas kernels, chunked_flow(): pl.pallas_call(functools.partial(flow_kernel, parts), in_specs=[anywhere,...  548 us

profile of v1, /device:TPU:15, one launch (start us, length us, event | category | flops | bytes accessed | tf_op | source)
XLA Modules:
  0.0 565.7 jit_solution(3053806096744915284)
XLA Ops:
  0.0 0.7 slice_add_fusion
  0.7 0.7 compare_convert_fusion.block_ref
  1.4 0.7 fusion.spread_ref
  2.1 547.9 %flow.1 = (bf16[3,8,512,512]{3,2,1,0:T(8,128)(2,1)}, bf16[2,3,32,128,256]{4,3,2,1,0:T(8,128)(2,1)}) custom-call(bf16[3,8,512,512]{3,2,1,0:T(8,128)(2,1)} %vertex_ref.1, bf16[3,8,512,512]{3,2,1,0:T(8,128)(2,1)} %loop_ref.1, f32[3,3]{1,0:T(4,128)} %own_ref.1, f32[3,3]{1,0:T(4,128)} %cross_ref.1, s32[1,512]{1,0:T(1,128)} %bitcast.3, s32[1,512]{1,0:T(1,128)} %bitcast.4, ...), custom_call_target="tpu_custom_call" | custom-call | tf_op jit(solution)/shard_map/flow/pallas_call | solution.py:750
  550.0 5.2 finish_tile.1
  555.2 10.4 %copy.11 = bf16[3,8,512,512]{3,2,1,0:T(8,128)(2,1)} copy(bf16[3,8,512,512]{3,2,1,0:T(8,128)(2,1)} %finish_tile.1) | data formatting | bytes 25165824
  (3 shorter events, 0.0 us)

commit v2 on v1

--- a/solution.py
+++ b/solution.py
@@ -348,6 +348,8 @@
 
 
 MESH = pl.DeviceIdType.MESH
+FLOW_LIMIT = 44 * 1024 * 1024
+LAST_LIMIT = 40 * 1024 * 1024
 
 
 def flow_kernel(
@@ -366,8 +368,6 @@
     wide_ref,
     vertex_buf,
     loop_buf,
-    base_buf,
-    tile_buf,
     pick_ref,
     spread_ref,
     block_ref,
@@ -378,7 +378,6 @@
     row_ref,
     col_ref,
     load_sem,
-    store_sem,
     self_sem,
     out_sem,
     in_sem,
@@ -414,10 +413,6 @@
             pltpu.make_async_copy(source.at[c, n], target.at[slot], load_sem.at[k, slot])
             for k, (source, target) in enumerate(((vertex_ref, vertex_buf), (loop_ref, loop_buf)))
         ]
-
-    def store(step, slot):
-        c, n = lax.div(step, mom_local), lax.rem(step, mom_local)
-        return pltpu.make_async_copy(base_buf.at[slot], base_ref.at[c, n], store_sem.at[slot])
 
     for copy in loads(0, 0):
         copy.start()
@@ -511,12 +506,7 @@
                 )
                 send_ref[k, c, :, rows, at * LANES : (at + 1) * LANES] = both.astype(bf16)
 
-        @pl.when(step >= 2)
-        def _():
-            store(step - 2, slot).wait()
-
-        base_buf[slot] = (product + vertex.astype(f32)).astype(bf16)
-        store(step, slot).start()
+        base_ref[c, n] = (product + vertex.astype(f32)).astype(bf16)
 
         @pl.when(step == part - 1)
         def _():
@@ -545,8 +535,6 @@
         return carry
 
     lax.fori_loop(0, chunks * channels, start_own, 0)
-    for step in (steps - 2, steps - 1):
-        store(step, step % 2).wait()
 
     def floor_div(value, by):
         return jnp.floor((value + 0.5) * (1.0 / by))
@@ -659,16 +647,9 @@
         k, d = lax.div(unit, channels), lax.rem(unit, channels)
         all_of(1, k, d).wait_recv()
         own_block(1, k, d).wait()
-        tiles = [
-            base_ref.at[d, :, :, pl.ds(pl.multiple_of(k * LANES + t * half, LANES), LANES)] for t in range(2)
-        ]
-        arrivals = [pltpu.make_async_copy(back_ref.at[k, d], recv_ref.at[0, 0], finish_sem.at[2])] + [
-            pltpu.make_async_copy(tiles[t], tile_buf.at[t], finish_sem.at[t]) for t in range(2)
-        ]
-        for copy in arrivals:
-            copy.start()
-        for copy in arrivals:
-            copy.wait()
+        arrival = pltpu.make_async_copy(back_ref.at[k, d], recv_ref.at[0, 0], finish_sem)
+        arrival.start()
+        arrival.wait()
 
         def finish_matrix(n, carry):
             rows = pl.ds(pl.multiple_of(n * pair, pair), pair)
@@ -680,15 +661,11 @@
                     piece = dot(spread_ref[...], piece.astype(bf16))
                 right = dot(piece[:, LANES:].astype(bf16), block_ref[k])
                 for t, add in enumerate((piece[:, :LANES], right)):
-                    tile_buf[t, n, there] = (tile_buf[t, n, there].astype(f32) + add).astype(bf16)
+                    cols = pl.ds(pl.multiple_of(k * LANES + t * half, LANES), LANES)
+                    base_ref[d, n, there, cols] = (base_ref[d, n, there, cols].astype(f32) + add).astype(bf16)
             return carry
 
         lax.fori_loop(0, mom_local, finish_matrix, 0)
-        departures = [pltpu.make_async_copy(tile_buf.at[t], tiles[t], finish_sem.at[t]) for t in range(2)]
-        for copy in departures:
-            copy.start()
-        for copy in departures:
-            copy.wait()
         return carry
 
     units = chunks * channels
@@ -703,32 +680,47 @@
     lax.fori_loop(0, units, drain, 0)
 
 
-def tile_finish_kernel(base_ref, received_ref, spread_ref, block_ref, out_ref):
-    places, depth = received_ref.shape[2:4]
-    batch, bonds = base_ref.shape[1:3]
+def last_kernel(base_ref, back_ref, partner_ref, out_ref, block_ref, tile_ref, in_sem, pass_sem, out_sem):
+    bf16, f32 = jnp.bfloat16, jnp.float32
+    chunks, channels, places, _, width = back_ref.shape
+    mom_local, bonds = base_ref.shape[1:3]
     half = bonds // 2
     group = half // places
     pair = 2 * group
-
-    def put(right):
-        for n in range(batch):
-            block = received_ref[0, 0, :, n * pair : (n + 1) * pair].astype(jnp.float32)
-            for s in range(2):
-                there = slice(s * half, (s + 1) * half)
-                piece = block[:, s * group : (s + 1) * group].reshape(half, LANES)
-                if s:
-                    piece = dot(spread_ref[...], piece.astype(jnp.bfloat16))
-                if right:
-                    piece = dot(piece.astype(jnp.bfloat16), block_ref[...])
-                out_ref[0, n, there] = (base_ref[0, n, there].astype(jnp.float32) + piece).astype(jnp.bfloat16)
-
-    @pl.when(pl.program_id(0) == 0)
-    def _():
-        put(False)
-
-    @pl.when(pl.program_id(0) == 1)
-    def _():
-        put(True)
+    d, edge = channels - 1, (chunks - 1) * LANES
+    arrival = pltpu.make_async_copy(back_ref.at[chunks - 1, d], block_ref, in_sem)
+    arrival.start()
+    done = [(base_ref.at[c], out_ref.at[c]) for c in range(d)]
+    for t in range(2):
+        if edge:
+            cols = pl.ds(t * half, edge)
+            done.append((base_ref.at[d, :, :, cols], out_ref.at[d, :, :, cols]))
+    passing = [pltpu.make_async_copy(*ends, pass_sem.at[at]) for at, ends in enumerate(done)]
+    for copy in passing:
+        copy.start()
+    down = lax.broadcasted_iota(jnp.int32, (half, half), 0)
+    spread = jnp.where(down == partner_ref[:, :half] - half, 1.0, 0.0).astype(bf16)
+    pick = jnp.where(down[:LANES, :LANES] + edge == partner_ref[:, half + edge :], 1.0, 0.0).astype(bf16)
+    arrival.wait()
+    leaving = []
+    for n in range(mom_local):
+        block = block_ref[:, n * pair : (n + 1) * pair].astype(f32)
+        for s in range(2):
+            there = slice(s * half, (s + 1) * half)
+            piece = block[:, s * group : (s + 1) * group].reshape(half, width)
+            if s:
+                piece = dot(spread, piece.astype(bf16))
+            right = dot(piece[:, LANES:].astype(bf16), pick)
+            for t, add in enumerate((piece[:, :LANES], right)):
+                cols = slice(t * half + edge, t * half + edge + LANES)
+                tile_ref[t, n, there] = (base_ref[d, n, there, cols].astype(f32) + add).astype(bf16)
+        for t in range(2):
+            cols = pl.ds(t * half + edge, LANES)
+            copy = pltpu.make_async_copy(tile_ref.at[t, n], out_ref.at[d, n, :, cols], out_sem.at[t, n])
+            copy.start()
+            leaving.append(copy)
+    for copy in passing + leaving:
+        copy.wait()
 
 
 def chunked_flow(vertex, loop_matrix, own_mix, cross_mix, shells, partner, grid_index):
@@ -750,10 +742,10 @@
     base, back = pl.pallas_call(
         functools.partial(flow_kernel, parts),
         in_specs=[anywhere, anywhere, scalars, scalars, inside, inside, inside],
-        out_specs=[anywhere, anywhere],
+        out_specs=[inside, anywhere],
         out_shape=[
-            jax.ShapeDtypeStruct(vertex.shape, bf16),
-            jax.ShapeDtypeStruct((chunks, channels, places, depth, width), bf16),
+            pltpu.VMEM(vertex.shape, bf16),
+            pltpu.HBM((chunks, channels, places, depth, width), bf16),
         ],
         scratch_shapes=[
             pltpu.VMEM((chunks, channels, places, depth, width), bf16),
@@ -761,8 +753,6 @@
             pltpu.VMEM((channels, 2, places * depth, LANES), f32),
             pltpu.VMEM((2, bonds, bonds), bf16),
             pltpu.VMEM((2, bonds, bonds), bf16),
-            pltpu.VMEM((2, bonds, bonds), bf16),
-            pltpu.VMEM((2, mom_local, bonds, LANES), bf16),
             pltpu.VMEM((half, half), bf16),
             pltpu.VMEM((half, half), bf16),
             pltpu.VMEM((chunks, LANES, LANES), bf16),
@@ -773,14 +763,13 @@
             pltpu.VMEM((2 * group, width), f32),
             pltpu.VMEM((chunks, 8, width), f32),
             dma((2, 2)),
-            dma((2,)),
             dma((units,)),
             dma((2, units)),
             dma((2, units)),
             dma((units,)),
-            dma((3,)),
+            dma(()),
         ],
-        compiler_params=pltpu.CompilerParams(collective_id=0, has_side_effects=True, vmem_limit_bytes=VMEM_LIMIT),
+        compiler_params=pltpu.CompilerParams(collective_id=0, has_side_effects=True, vmem_limit_bytes=FLOW_LIMIT),
         name="flow",
     )(
         vertex,
@@ -792,30 +781,21 @@
         grid_index.reshape(1, count),
     )
 
-    lower_partner = partner[:half] - half
-    uppers = jnp.arange(half, dtype=jnp.int32)
-    spread = (lower_partner[None, :] == uppers[:, None]).astype(bf16)
-    edge = (chunks - 1) * LANES
-    block = (lower_partner[edge:, None] - edge == uppers[None, :LANES]).astype(bf16)
-    batch = math.gcd(mom_local, 4)
-    tile = pl.BlockSpec((1, batch, bonds, LANES), lambda t, i: (channels - 1, i, 0, chunks - 1 + t * chunks))
     return pl.pallas_call(
-        tile_finish_kernel,
-        grid=(2, mom_local // batch),
-        in_specs=[
-            tile,
-            pl.BlockSpec(
-                (1, 1, places, batch * 2 * group, LANES), lambda t, i: (chunks - 1, channels - 1, 0, i, t)
-            ),
-            whole((half, half)),
-            whole((LANES, LANES)),
+        last_kernel,
+        in_specs=[inside, anywhere, inside],
+        out_specs=anywhere,
+        out_shape=pltpu.HBM(vertex.shape, bf16),
+        scratch_shapes=[
+            pltpu.VMEM((places, depth, width), bf16),
+            pltpu.VMEM((2, mom_local, bonds, LANES), bf16),
+            dma(()),
+            dma((channels + 1,)),
+            dma((2, mom_local)),
         ],
-        out_specs=tile,
-        out_shape=jax.ShapeDtypeStruct(vertex.shape, bf16),
-        input_output_aliases={0: 0},
-        compiler_params=params(2),
-        name="finish_tile",
-    )(base, back, spread, block)
+        compiler_params=pltpu.CompilerParams(vmem_limit_bytes=LAST_LIMIT),
+        name="finish_last_unit",
+    )(base, back, partner.reshape(1, bonds))
 
 
 def per_device(vertex, *others):

time: 567 us -> 554 us (0.977)
  local copies, waits for them, and re-layouts: 10.4 us -> 0.01 us
    unnamed x1 -> x2, local copies, waits for them, and re-layouts: 10.4 us -> 0.01 us
where the time goes in v2:
time: 554 us; the launch traced here: 553 us
  Pallas kernels  553 us (100%)
    pallas_call x1, Pallas kernels, chunked_flow(): pl.pallas_call(functools.partial(flow_kernel, parts), in_specs=[anywhere,...  548 us

profile of v2, /device:TPU:15, one launch (start us, length us, event | category | flops | bytes accessed | tf_op | source)
XLA Modules:
  0.0 552.8 jit_solution(12040016358748295315)
XLA Ops:
  0.0 0.0 copy-start
  0.0 547.8 %flow.1 = (bf16[3,8,512,512]{3,2,1,0:T(8,128)(2,1)S(1)}, bf16[2,3,32,128,256]{4,3,2,1,0:T(8,128)(2,1)}) custom-call(bf16[3,8,512,512]{3,2,1,0:T(8,128)(2,1)} %vertex_ref.1, bf16[3,8,512,512]{3,2,1,0:T(8,128)(2,1)} %loop_ref.1, f32[3,3]{1,0:T(4,128)} %own_ref.1, f32[3,3]{1,0:T(4,128)} %cross_ref.1, s32[1,512]{1,0:T(1,128)} %bitcast.3, s32[1,512]{1,0:T(1,128)} %bitcast.5, ...), custom_call_target="tpu_custom_call" | custom-call | tf_op jit(solution)/shard_map/flow/pallas_call | solution.py:742
  547.8 0.0 copy-done
  547.8 5.0 finish_last_unit.1
Async XLA Ops:
  0.0 547.8 %copy-start = (s32[512]{0:T(512)S(1)}, s32[512]{0:T(512)}, u32[]{:S(2)}) copy-start(s32[512]{0:T(512)} %param.12) | copy-start | bytes 6148

commit v3 on v2

--- a/solution.py
+++ b/solution.py
@@ -349,7 +349,7 @@
 
 MESH = pl.DeviceIdType.MESH
 FLOW_LIMIT = 44 * 1024 * 1024
-LAST_LIMIT = 40 * 1024 * 1024
+LAST_LIMIT = 16 * 1024 * 1024
 
 
 def flow_kernel(
@@ -363,6 +363,7 @@
     grid_ref,
     base_ref,
     back_ref,
+    tail_ref,
     send_ref,
     recv_ref,
     wide_ref,
@@ -402,10 +403,9 @@
     barrier = pltpu.get_barrier_semaphore()
 
     def greet(offset, carry):
-        pl.semaphore_signal(barrier, inc=1, device_id=device(offset)[1], device_id_type=MESH)
+        far = lax.rem(offset + places // 2 - 2, places - 1) + 1
+        pl.semaphore_signal(barrier, inc=1, device_id=device(far)[1], device_id_type=MESH)
         return carry
-
-    lax.fori_loop(1, places, greet, 0)
 
     def loads(step, slot):
         c, n = lax.div(step, mom_local), lax.rem(step, mom_local)
@@ -416,7 +416,7 @@
 
     for copy in loads(0, 0):
         copy.start()
-
+    lax.fori_loop(1, places, greet, 0)
     down = lax.broadcasted_iota(jnp.int32, (half, half), 0)
     lower_partner = partner_ref[:, :half] - half
     pick_ref[...] = jnp.where(down == partner_ref[:, half:], 1.0, 0.0).astype(bf16)
@@ -440,14 +440,14 @@
 
         lax.fori_loop(1, places, one, 0)
 
-    def backward(unit_k, unit_c):
+    def backward(unit_k, unit_c, landing):
         unit = unit_k * channels + unit_c
 
         def one(offset, carry):
             at, target = device(offset)
             pltpu.make_async_remote_copy(
                 src_ref=send_ref.at[unit_k, unit_c, at],
-                dst_ref=back_ref.at[unit_k, unit_c, place],
+                dst_ref=landing.at[place],
                 send_sem=out_sem.at[1, unit],
                 recv_sem=in_sem.at[1, unit],
                 device_id=target,
@@ -457,23 +457,28 @@
 
         lax.fori_loop(1, places, one, 0)
 
+    def landing_of(way, unit_k, unit_c):
+        if way == 2:
+            return tail_ref
+        return (back_ref if way else recv_ref).at[unit_k, unit_c]
+
     def all_of(way, unit_k, unit_c):
         unit = unit_k * channels + unit_c
-        landing = back_ref if way else recv_ref
         return pltpu.make_async_remote_copy(
             src_ref=send_ref.at[unit_k, unit_c, pl.ds(0, places - 1)],
-            dst_ref=landing.at[unit_k, unit_c, pl.ds(0, places - 1)],
-            send_sem=out_sem.at[way, unit],
-            recv_sem=in_sem.at[way, unit],
+            dst_ref=landing_of(way, unit_k, unit_c).at[pl.ds(0, places - 1)],
+            send_sem=out_sem.at[min(way, 1), unit],
+            recv_sem=in_sem.at[min(way, 1), unit],
             device_id=device(1)[1],
             device_id_type=MESH,
         )
 
     def own_block(way, unit_k, unit_c):
         unit = unit_k * channels + unit_c
-        landing, sem = (back_ref, home_sem) if way else (recv_ref, self_sem)
         return pltpu.make_async_copy(
-            send_ref.at[unit_k, unit_c, place], landing.at[unit_k, unit_c, place], sem.at[unit]
+            send_ref.at[unit_k, unit_c, place],
+            landing_of(way, unit_k, unit_c).at[place],
+            (home_sem if way else self_sem).at[unit],
         )
 
     part = mom_local // parts
@@ -635,10 +640,20 @@
             return carry
 
         lax.fori_loop(0, places, narrow, 0)
-        for d in range(channels):
-            backward(k, d)
-        for d in range(channels):
+        for d in range(channels - 1):
+            backward(k, d, back_ref.at[k, d])
             own_block(1, k, d).start()
+
+        @pl.when(k < chunks - 1)
+        def _():
+            backward(k, channels - 1, back_ref.at[k, channels - 1])
+            own_block(1, k, channels - 1).start()
+
+        @pl.when(k == chunks - 1)
+        def _():
+            backward(k, channels - 1, tail_ref)
+            own_block(2, k, channels - 1).start()
+
         return carry
 
     lax.fori_loop(0, chunks, lattice_chunk, 0)
@@ -670,8 +685,8 @@
 
     units = chunks * channels
     lax.fori_loop(0, units - 1, finish_unit, 0)
-    all_of(1, chunks - 1, channels - 1).wait_recv()
-    own_block(1, chunks - 1, channels - 1).wait()
+    all_of(2, chunks - 1, channels - 1).wait_recv()
+    own_block(2, chunks - 1, channels - 1).wait()
 
     def drain(unit, carry):
         all_of(1, lax.div(unit, channels), lax.rem(unit, channels)).wait_send()
@@ -680,16 +695,15 @@
     lax.fori_loop(0, units, drain, 0)
 
 
-def last_kernel(base_ref, back_ref, partner_ref, out_ref, block_ref, tile_ref, in_sem, pass_sem, out_sem):
+def last_kernel(base_ref, block_ref, partner_ref, out_ref, tile_ref, pass_sem, out_sem):
     bf16, f32 = jnp.bfloat16, jnp.float32
-    chunks, channels, places, _, width = back_ref.shape
-    mom_local, bonds = base_ref.shape[1:3]
+    places, _, width = block_ref.shape
+    channels, mom_local, bonds = base_ref.shape[:3]
     half = bonds // 2
+    chunks = half // LANES
     group = half // places
     pair = 2 * group
     d, edge = channels - 1, (chunks - 1) * LANES
-    arrival = pltpu.make_async_copy(back_ref.at[chunks - 1, d], block_ref, in_sem)
-    arrival.start()
     done = [(base_ref.at[c], out_ref.at[c]) for c in range(d)]
     for t in range(2):
         if edge:
@@ -701,7 +715,6 @@
     down = lax.broadcasted_iota(jnp.int32, (half, half), 0)
     spread = jnp.where(down == partner_ref[:, :half] - half, 1.0, 0.0).astype(bf16)
     pick = jnp.where(down[:LANES, :LANES] + edge == partner_ref[:, half + edge :], 1.0, 0.0).astype(bf16)
-    arrival.wait()
     leaving = []
     for n in range(mom_local):
         block = block_ref[:, n * pair : (n + 1) * pair].astype(f32)
@@ -739,13 +752,14 @@
     scalars = pl.BlockSpec(memory_space=pltpu.SMEM)
     inside = pl.BlockSpec(memory_space=pltpu.VMEM)
     dma = pltpu.SemaphoreType.DMA
-    base, back = pl.pallas_call(
+    base, _, tail = pl.pallas_call(
         functools.partial(flow_kernel, parts),
         in_specs=[anywhere, anywhere, scalars, scalars, inside, inside, inside],
-        out_specs=[inside, anywhere],
+        out_specs=[inside, anywhere, inside],
         out_shape=[
             pltpu.VMEM(vertex.shape, bf16),
             pltpu.HBM((chunks, channels, places, depth, width), bf16),
+            pltpu.VMEM((places, depth, width), bf16),
         ],
         scratch_shapes=[
             pltpu.VMEM((chunks, channels, places, depth, width), bf16),
@@ -783,19 +797,17 @@
 
     return pl.pallas_call(
         last_kernel,
-        in_specs=[inside, anywhere, inside],
+        in_specs=[inside, inside, inside],
         out_specs=anywhere,
         out_shape=pltpu.HBM(vertex.shape, bf16),
         scratch_shapes=[
-            pltpu.VMEM((places, depth, width), bf16),
             pltpu.VMEM((2, mom_local, bonds, LANES), bf16),
-            dma(()),
             dma((channels + 1,)),
             dma((2, mom_local)),
         ],
         compiler_params=pltpu.CompilerParams(vmem_limit_bytes=LAST_LIMIT),
         name="finish_last_unit",
-    )(base, back, partner.reshape(1, bonds))
+    )(base, tail, partner.reshape(1, bonds))
 
 
 def per_device(vertex, *others):

time: 554 us -> 553 us (level)
  no operation moved by 1% of the time
where the time goes in v3:
time: 553 us; the launch traced here: 552 us
  Pallas kernels  552 us (100%)
    pallas_call x1, Pallas kernels, chunked_flow(): pl.pallas_call(functools.partial(flow_kernel, parts), in_specs=[anywhere,...  548 us

profile of v3, /device:TPU:15, one launch (start us, length us, event | category | flops | bytes accessed | tf_op | source)
XLA Modules:
  0.0 552.2 jit_solution(14427219874706730745)
XLA Ops:
  0.0 0.0 copy-start
  0.0 547.5 %flow.1 = (bf16[3,8,512,512]{3,2,1,0:T(8,128)(2,1)S(1)}, bf16[2,3,32,128,256]{4,3,2,1,0:T(8,128)(2,1)}, bf16[32,128,256]{2,1,0:T(8,128)(2,1)S(1)}) custom-call(bf16[3,8,512,512]{3,2,1,0:T(8,128)(2,1)} %vertex_ref.1, bf16[3,8,512,512]{3,2,1,0:T(8,128)(2,1)} %loop_ref.1, f32[3,3]{1,0:T(4,128)} %own_ref.1, f32[3,3]{1,0:T(4,128)} %cross_ref.1, ...), custom_call_target="tpu_custom_call" | custom-call | tf_op jit(solution)/shard_map/flow/pallas_call | solution.py:755
  547.5 0.0 copy-done
  547.6 4.7 finish_last_unit.1
Async XLA Ops:
  0.0 547.5 %copy-start = (s32[512]{0:T(512)S(1)}, s32[512]{0:T(512)}, u32[]{:S(2)}) copy-start(s32[512]{0:T(512)} %param.12) | copy-start | bytes 6148

commit v4 on v3

--- a/solution.py
+++ b/solution.py
@@ -705,10 +705,6 @@
     pair = 2 * group
     d, edge = channels - 1, (chunks - 1) * LANES
     done = [(base_ref.at[c], out_ref.at[c]) for c in range(d)]
-    for t in range(2):
-        if edge:
-            cols = pl.ds(t * half, edge)
-            done.append((base_ref.at[d, :, :, cols], out_ref.at[d, :, :, cols]))
     passing = [pltpu.make_async_copy(*ends, pass_sem.at[at]) for at, ends in enumerate(done)]
     for copy in passing:
         copy.start()
@@ -726,12 +722,13 @@
             right = dot(piece[:, LANES:].astype(bf16), pick)
             for t, add in enumerate((piece[:, :LANES], right)):
                 cols = slice(t * half + edge, t * half + edge + LANES)
-                tile_ref[t, n, there] = (base_ref[d, n, there, cols].astype(f32) + add).astype(bf16)
-        for t in range(2):
-            cols = pl.ds(t * half + edge, LANES)
-            copy = pltpu.make_async_copy(tile_ref.at[t, n], out_ref.at[d, n, :, cols], out_sem.at[t, n])
-            copy.start()
-            leaving.append(copy)
+                tile_ref[n, there, cols] = (base_ref[d, n, there, cols].astype(f32) + add).astype(bf16)
+                if edge:
+                    kept = slice(t * half, t * half + edge)
+                    tile_ref[n, there, kept] = base_ref[d, n, there, kept]
+        copy = pltpu.make_async_copy(tile_ref.at[n], out_ref.at[d, n], out_sem.at[n])
+        copy.start()
+        leaving.append(copy)
     for copy in passing + leaving:
         copy.wait()
 
@@ -801,9 +798,9 @@
         out_specs=anywhere,
         out_shape=pltpu.HBM(vertex.shape, bf16),
         scratch_shapes=[
-            pltpu.VMEM((2, mom_local, bonds, LANES), bf16),
-            dma((channels + 1,)),
-            dma((2, mom_local)),
+            pltpu.VMEM((mom_local, bonds, bonds), bf16),
+            dma((channels,)),
+            dma((mom_local,)),
         ],
         compiler_params=pltpu.CompilerParams(vmem_limit_bytes=LAST_LIMIT),
         name="finish_last_unit",

time: 553 us -> 553 us (level)
  no operation moved by 1% of the time
where the time goes in v4:
time: 553 us; the launch traced here: 552 us
  Pallas kernels  552 us (100%)
    pallas_call x1, Pallas kernels, chunked_flow(): pl.pallas_call(functools.partial(flow_kernel, parts), in_specs=[anywhere,...  548 us

profile of v4, /device:TPU:15, one launch (start us, length us, event | category | flops | bytes accessed | tf_op | source)
XLA Modules:
  0.0 552.2 jit_solution(2427406428806926072)
XLA Ops:
  0.0 0.0 copy-start
  0.0 547.5 %flow.1 = (bf16[3,8,512,512]{3,2,1,0:T(8,128)(2,1)S(1)}, bf16[2,3,32,128,256]{4,3,2,1,0:T(8,128)(2,1)}, bf16[32,128,256]{2,1,0:T(8,128)(2,1)S(1)}) custom-call(bf16[3,8,512,512]{3,2,1,0:T(8,128)(2,1)} %vertex_ref.1, bf16[3,8,512,512]{3,2,1,0:T(8,128)(2,1)} %loop_ref.1, f32[3,3]{1,0:T(4,128)} %own_ref.1, f32[3,3]{1,0:T(4,128)} %cross_ref.1, ...), custom_call_target="tpu_custom_call" | custom-call | tf_op jit(solution)/shard_map/flow/pallas_call | solution.py:752
  547.5 0.0 copy-done
  547.6 4.6 finish_last_unit.1
Async XLA Ops:
  0.0 547.5 %copy-start = (s32[512]{0:T(512)S(1)}, s32[512]{0:T(512)}, u32[]{:S(2)}) copy-start(s32[512]{0:T(512)} %param.12) | copy-start | bytes 6148

commit v5 on v4

--- a/solution.py
+++ b/solution.py
@@ -704,7 +704,7 @@
     group = half // places
     pair = 2 * group
     d, edge = channels - 1, (chunks - 1) * LANES
-    done = [(base_ref.at[c], out_ref.at[c]) for c in range(d)]
+    done = [(base_ref.at[pl.ds(0, d)], out_ref.at[pl.ds(0, d)])] if d else []
     passing = [pltpu.make_async_copy(*ends, pass_sem.at[at]) for at, ends in enumerate(done)]
     for copy in passing:
         copy.start()

time: 553 us -> 553 us (level)
  no operation moved by 1% of the time
where the time goes in v5:
time: 553 us; the launch traced here: 552 us
  Pallas kernels  552 us (100%)
    pallas_call x1, Pallas kernels, chunked_flow(): pl.pallas_call(functools.partial(flow_kernel, parts), in_specs=[anywhere,...  548 us

profile of v5, /device:TPU:15, one launch (start us, length us, event | category | flops | bytes accessed | tf_op | source)
XLA Modules:
  0.0 552.3 jit_solution(5221735024559136213)
XLA Ops:
  0.0 0.0 copy-start
  0.0 547.5 %flow.1 = (bf16[3,8,512,512]{3,2,1,0:T(8,128)(2,1)S(1)}, bf16[2,3,32,128,256]{4,3,2,1,0:T(8,128)(2,1)}, bf16[32,128,256]{2,1,0:T(8,128)(2,1)S(1)}) custom-call(bf16[3,8,512,512]{3,2,1,0:T(8,128)(2,1)} %vertex_ref.1, bf16[3,8,512,512]{3,2,1,0:T(8,128)(2,1)} %loop_ref.1, f32[3,3]{1,0:T(4,128)} %own_ref.1, f32[3,3]{1,0:T(4,128)} %cross_ref.1, ...), custom_call_target="tpu_custom_call" | custom-call | tf_op jit(solution)/shard_map/flow/pallas_call | solution.py:752
  547.5 0.0 copy-done
  547.6 4.8 finish_last_unit.1
Async XLA Ops:
  0.0 547.5 %copy-start = (s32[512]{0:T(512)S(1)}, s32[512]{0:T(512)}, u32[]{:S(2)}) copy-start(s32[512]{0:T(512)} %param.12) | copy-start | bytes 6148
